TPU v7x, 128 devices: a whole 4x4x4 slice. The times are simulated.
128 devices in a mesh: leaf: 32 (over z, y, core), rows: 4 (over x).
Axes of the slice: x: 4, y: 4, z: 4, core: 2. Of those that a mesh axis runs over, the one named last changes fastest.
Arguments:
- child_update: float32 [32, 512, 512], P('leaf', 'rows'), as said below
- block_maps: int32 [3, 32, 4], replicated, may hold values from 0 to 11, as said below
- sep_share: float32 [32, 3, 1024, 1024], P('leaf', None, 'rows'), as said below
- coupling_share: float32 [32, 3, 512, 1024], P('leaf', None, 'rows')
Outputs:
- diag_factor: float32 [32, 3, 1024, 1024], P('leaf', None, 'rows')
- below_factor: float32 [32, 3, 512, 1024], P('leaf', None, 'rows')
- top_update: float32 [32, 512, 512], P('leaf', 'rows')
Inputs may be any that keep to these rules, and one draw needn't show every extreme that they name: Each row block_maps[k, c] names 4 different front blocks; at every level k, the rows 2g and 2g+1 together name every block from 8 on. At level k only the rows c < 32 / 2^k are used. `child_update`: Symmetric. `sep_share`: symmetric in its last two dimensions.
All inputs are finite; a program needn't handle non-finite values.
Results may differ from a plain program's by a relative error of at most 0.00012.
Values sent between devices are 32-bit elements; how exact they have to be, the bound alone decides.
No kernel may reach another device: no remote copies, remote signals or barrier semaphores. Data moves between devices by JAX's collectives and lax.ppermute only.
A program may use at most 192 MiB of HBM per device.

v0:
```python
import jax
import jax.numpy as jnp
from jax import lax
from jax.sharding import PartitionSpec as P

BLK = 128
LEVELS = 3
highest = lax.Precision.HIGHEST


def partner(x, axis, stride):
    return lax.ppermute(x, axis, [(i, i ^ 1 << stride) for i in range(lax.axis_size(axis))])


def block_cholesky(matrix):
    order = matrix.shape[-1]
    if order <= 512:
        return jnp.linalg.cholesky(matrix, symmetrize_input=False)
    half = order // 2
    top_factor = block_cholesky(matrix[:half, :half])
    lower_panel = lax.linalg.triangular_solve(
        top_factor, matrix[half:, :half], left_side=False, lower=True, transpose_a=True
    )
    remainder = matrix[half:, half:] - jnp.dot(
        lower_panel, lower_panel.T, precision=highest, preferred_element_type=jnp.float32
    )
    bottom_factor = block_cholesky(remainder)
    upper_zero = jnp.zeros((half, order - half), jnp.float32)
    top_rows = jnp.concatenate([top_factor, upper_zero], axis=1)
    bottom_rows = jnp.concatenate([lower_panel, bottom_factor], axis=1)
    return jnp.concatenate([top_rows, bottom_rows], axis=0)


def sym_cholesky(matrix):
    return block_cholesky((matrix + matrix.T) * 0.5)


def place_columns(portion, block_map, blocks_front):
    count_rows = portion.shape[0]
    blocks_child = block_map.shape[0]
    selector = (block_map[None, :] == jnp.arange(blocks_front, dtype=jnp.int32)[:, None]).astype(
        jnp.float32
    )
    placed = jnp.einsum(
        "qm,nmb->nqb", selector, portion.reshape(count_rows, blocks_child, BLK), precision=highest
    )
    return placed.reshape(count_rows, blocks_front * BLK)


def pick_rows(portion, block_map, global_rows):
    count_rows = portion.shape[0]
    blocks_child = block_map.shape[0]
    matches = (block_map[None, :] == (global_rows // BLK)[:, None]).astype(jnp.int32)
    found = jnp.sum(matches, axis=1) > 0
    source_block = jnp.sum(matches * jnp.arange(blocks_child, dtype=jnp.int32)[None, :], axis=1)
    source_row = source_block * BLK + global_rows % BLK
    usable = found & (source_row >= 0) & (source_row < count_rows)
    picked = jnp.take(portion, jnp.clip(source_row, 0, count_rows - 1), axis=0)
    return jnp.where(usable[:, None], picked, 0.0)


def on_device(child_update, block_maps, sep_share, coupling_share):
    upd_rows = child_update.shape[1]
    upd_width = child_update.shape[2]
    sep_rows = sep_share.shape[2]
    sep_width = sep_share.shape[3]
    front_width = sep_width + upd_width
    blocks_front = front_width // BLK
    leaf_index = lax.axis_index("leaf")
    row_id = lax.axis_index("rows")
    targets = jnp.concatenate(
        [
            row_id * sep_rows + jnp.arange(sep_rows, dtype=jnp.int32),
            sep_width + row_id * upd_rows + jnp.arange(upd_rows, dtype=jnp.int32),
        ]
    )
    current = child_update[0]
    pend_sep = sep_share[0]
    pend_cpl = coupling_share[0]
    diag_parts = []
    below_parts = []
    for level_index in range(LEVELS):
        partner_rows, got_sep, got_cpl = partner((current, pend_sep, pend_cpl), "leaf", level_index)
        pend_sep = pend_sep + got_sep
        pend_cpl = pend_cpl + got_cpl
        sep_orig = pend_sep[0]
        cpl_orig = pend_cpl[0]
        pend_sep = pend_sep[1:]
        pend_cpl = pend_cpl[1:]
        is_right = leaf_index >> level_index & 1
        left_rows = jnp.where(is_right == 0, current, partner_rows)
        right_rows = jnp.where(is_right == 0, partner_rows, current)
        first_child = (leaf_index >> level_index + 1) * 2
        left_map = lax.dynamic_index_in_dim(block_maps[level_index], first_child, 0, keepdims=False)
        right_map = lax.dynamic_index_in_dim(
            block_maps[level_index], first_child + 1, 0, keepdims=False
        )

        def add_children(running, portions, offset, left_map=left_map, right_map=right_map):
            for portion, block_map in ((portions[0], left_map), (portions[1], right_map)):
                running = running + place_columns(
                    pick_rows(portion, block_map, targets), block_map, blocks_front
                )
            return running

        front_rows = add_children(
            jnp.zeros((sep_rows + upd_rows, front_width), jnp.float32),
            (
                lax.all_gather(left_rows, "rows", axis=0, tiled=True),
                lax.all_gather(right_rows, "rows", axis=0, tiled=True),
            ),
            jnp.int32(0),
        )
        front_pivot = front_rows[:sep_rows, :sep_width] + sep_orig
        front_below = front_rows[sep_rows:, :sep_width] + cpl_orig
        front_trail = front_rows[sep_rows:, sep_width:]
        pivot_block = lax.all_gather(front_pivot, "rows", axis=0, tiled=True)
        pivot_factor = sym_cholesky(pivot_block)
        solved = lax.linalg.triangular_solve(
            pivot_factor, front_below, left_side=False, lower=True, transpose_a=True
        )
        left_part = solved

        def product(portion, offset, left_part=left_part):
            return -jnp.dot(
                left_part, portion.T, precision=highest, preferred_element_type=jnp.float32
            )

        schur_part = front_trail + product(
            lax.all_gather(solved, "rows", axis=0, tiled=True), jnp.int32(0)
        )
        diag_parts.append(lax.dynamic_slice_in_dim(pivot_factor, row_id * sep_rows, sep_rows, 0))
        below_parts.append(solved)
        current = schur_part
    return (jnp.stack(diag_parts)[None], jnp.stack(below_parts)[None], current[None])


def solution(mesh):
    return jax.shard_map(
        on_device,
        mesh=mesh,
        in_specs=(
            P("leaf", "rows", None),
            P(),
            P("leaf", None, "rows", None),
            P("leaf", None, "rows", None),
        ),
        out_specs=(
            P("leaf", None, "rows", None),
            P("leaf", None, "rows", None),
            P("leaf", "rows", None),
        ),
        check_vma=False,
    )
```

profile of v0, /device:TPU:0, one launch (start us, length us, event | category | flops | bytes accessed | tf_op | source)
XLA Modules:
  0.0 1728.3 jit_solution(13907045781276301136)
XLA Ops:
  16.0 21.4 %all-gather.15.cloned.1.call-done = f32[512,512]{1,0:T(8,128)} async-done(((f32[128,512]{1,0:T(8,128)}), f32[512,512]{1,0:T(8,128)}) %all-gather.15.cloned.1.call-update) | async-done | bytes 1048592 | tf_op jit(solution)/shard_map/all_gather | solution.py:110
  42.0 21.4 %all-gather.13.cloned.1.call-done = f32[512,512]{1,0:T(8,128)} async-done(((f32[128,512]{1,0:T(8,128)}), f32[512,512]{1,0:T(8,128)}) %all-gather.13.cloned.1.call-update) | async-done | bytes 1048592 | tf_op jit(solution)/shard_map/all_gather | solution.py:109
  91.2 36.7 %all-gather.17.cloned.1.call-done = f32[1024,1024]{0,1:T(8,128)} async-done(((f32[256,1024]{0,1:T(8,128)}), f32[1024,1024]{0,1:T(8,128)}) %all-gather.17.cloned.1.call-update) | async-done | bytes 4194320 | tf_op jit(solution)/shard_map/all_gather | solution.py:117
  140.2 11.7 cholesky.645
  165.9 11.7 cholesky.665
  220.3 12.1 cholesky.703
  239.0 11.9 while.12
  251.6 40.1 %custom-call.48 = f32[4,128,128]{1,2,0:T(8,128)S(1)} custom-call(f32[4,128,128]{2,1,0:T(8,128)} %copy-done.32), custom_call_target="InvertDiagBlocksLowerTriangular" | custom-call | tf_op jit(solution)/shard_map/triangular_solve/custom-call.3 | solution.py:21
  340.0 12.5 cholesky.738
  372.0 13.2 cholesky.759
  426.6 28.5 %while.13 = (s32[]{:T(128)}, f32[1024,1024]{1,0:T(8,128)}, s32[8,2]{0,1:T(2,128)S(1)}, f32[8,128,128]{2,1,0:T(8,128)}, s32[]{:T(128)}) while((s32[]{:T(128)}, f32[1024,1024]{1,0:T(8,128)}, s32[8,2]{0,1:T(2,128)S(1)}, f32[8,128,128]{2,1,0:T(8,128)}, s32[]{:T(128)}) %tuple.250), condition=%wide.while_cond.1, body=%wide.while_body.1.sunk | while | flops 2 | bytes 132205 | solution.py:119
  455.0 80.2 %custom-call.52 = f32[8,128,128]{1,2,0:T(8,128)} custom-call(f32[8,128,128]{2,1,0:T(8,128)} %get-tuple-element.48), custom_call_target="InvertDiagBlocksLowerTriangular" | custom-call | tf_op jit(solution)/shard_map/triangular_solve/custom-call.8 | solution.py:119
  559.0 34.9 %all-gather.19.cloned.1.call-done = f32[512,1024]{0,1:T(8,128)} async-done(((f32[128,1024]{0,1:T(8,128)}), f32[512,1024]{0,1:T(8,128)}) %all-gather.19.cloned.1.call-update) | async-done | bytes 2097168 | tf_op jit(solution)/shard_map/all_gather | solution.py:130
  611.4 44.2 %collective-permute-done.4 = f32[2,256,1024]{1,2,0:T(8,128)} collective-permute-done((f32[2,256,1024]{1,2,0:T(8,128)}, f32[2,256,1024]{1,2,0:T(8,128)}, u32[]{:S(2)}, u32[]{:S(2)}) %collective-permute-start.4) | collective-permute-done | bytes 2097184 | tf_op jit(solution)/shard_map/ppermute | solution.py:12
  681.9 22.8 %collective-permute-done.5 = f32[2,128,1024]{1,2,0:T(8,128)S(1)} collective-permute-done((f32[2,128,1024]{1,2,0:T(8,128)}, f32[2,128,1024]{1,2,0:T(8,128)S(1)}, u32[]{:S(2)}, u32[]{:S(2)}) %collective-permute-start.5) | collective-permute-done | bytes 1048608 | tf_op jit(solution)/shard_map/ppermute | solution.py:12
  708.9 18.6 %all-gather.25.cloned.1.call-done = f32[1024,1024]{0,1:T(8,128)} async-done(((f32[256,1024]{0,1:T(8,128)}), f32[1024,1024]{0,1:T(8,128)}) %all-gather.25.cloned.1.call-update) | async-done | bytes 4194320 | tf_op jit(solution)/shard_map/all_gather | solution.py:117
  764.7 12.3 cholesky.811
  814.7 12.1 cholesky.849
  842.9 39.3 %custom-call.56 = f32[4,128,128]{1,2,0:T(8,128)S(1)} custom-call(f32[4,128,128]{2,1,0:T(8,128)S(1)} %get-tuple-element.49), custom_call_target="InvertDiagBlocksLowerTriangular" | custom-call | tf_op jit(solution)/shard_map/triangular_solve/custom-call.3 | solution.py:21
  922.7 12.5 cholesky.884
  949.9 13.2 cholesky.905
  1000.6 23.2 %while.15 = (s32[]{:T(128)}, f32[1024,1024]{1,0:T(8,128)}, s32[8,2]{0,1:T(2,128)S(1)}, f32[8,128,128]{2,1,0:T(8,128)S(1)}, s32[]{:T(128)}) while((s32[]{:T(128)}, f32[1024,1024]{1,0:T(8,128)}, s32[8,2]{0,1:T(2,128)S(1)}, f32[8,128,128]{2,1,0:T(8,128)S(1)}, s32[]{:T(128)}) %tuple.291), condition=%wide.while_cond.1.clone, body=%wide.while_body.1.clone.sunk | while | flops 2 | bytes 131189 | solution.py:119
  1023.9 79.6 %custom-call.60 = f32[8,128,128]{1,2,0:T(8,128)} custom-call(f32[8,128,128]{2,1,0:T(8,128)S(1)} %get-tuple-element.50), custom_call_target="InvertDiagBlocksLowerTriangular" | custom-call | tf_op jit(solution)/shard_map/triangular_solve/custom-call.8 | solution.py:119
  1122.9 35.0 %all-gather.27.cloned.1.call-done = f32[512,1024]{0,1:T(8,128)} async-done(((f32[128,1024]{0,1:T(8,128)}), f32[512,1024]{0,1:T(8,128)}) %all-gather.27.cloned.1.call-update) | async-done | bytes 2097168 | tf_op jit(solution)/shard_map/all_gather | solution.py:130
  1177.5 22.2 %all-gather.31.cloned.1.call-done = f32[512,512]{0,1:T(8,128)} async-done(((f32[128,512]{0,1:T(8,128)}), f32[512,512]{0,1:T(8,128)}) %all-gather.31.cloned.1.call-update) | async-done | bytes 1048592 | tf_op jit(solution)/shard_map/all_gather | solution.py:110
  1206.1 21.9 %all-gather.29.cloned.1.call-done = f32[512,512]{0,1:T(8,128)} async-done(((f32[128,512]{0,1:T(8,128)}), f32[512,512]{0,1:T(8,128)}) %all-gather.29.cloned.1.call-update) | async-done | bytes 1048592 | tf_op jit(solution)/shard_map/all_gather | solution.py:109
  1264.9 33.0 %all-gather.33.cloned.1.call-done = f32[1024,1024]{0,1:T(8,128)} async-done(((f32[256,1024]{0,1:T(8,128)}), f32[1024,1024]{0,1:T(8,128)}) %all-gather.33.cloned.1.call-update) | async-done | bytes 4194320 | tf_op jit(solution)/shard_map/all_gather | solution.py:117
  1393.4 11.9 cholesky.995
  1421.2 39.3 %custom-call.64 = f32[4,128,128]{1,2,0:T(8,128)S(1)} custom-call(f32[4,128,128]{2,1,0:T(8,128)S(1)} %get-tuple-element.51), custom_call_target="InvertDiagBlocksLowerTriangular" | custom-call | tf_op jit(solution)/shard_map/triangular_solve/custom-call.3 | solution.py:21
  1565.7 23.2 %while.17 = (s32[]{:T(128)}, f32[1024,1024]{1,0:T(8,128)}, s32[8,2]{0,1:T(2,128)S(1)}, f32[8,128,128]{2,1,0:T(8,128)S(1)}, s32[]{:T(128)}) while((s32[]{:T(128)}, f32[1024,1024]{1,0:T(8,128)}, s32[8,2]{0,1:T(2,128)S(1)}, f32[8,128,128]{2,1,0:T(8,128)S(1)}, s32[]{:T(128)}) %tuple.292), condition=%wide.while_cond.1.clone.1, body=%wide.while_body.1.clone.1.sunk | while | flops 2 | bytes 131189 | solution.py:119
  1588.9 78.8 %custom-call.68 = f32[8,128,128]{1,2,0:T(8,128)S(1)} custom-call(f32[8,128,128]{2,1,0:T(8,128)S(1)} %get-tuple-element.52), custom_call_target="InvertDiagBlocksLowerTriangular" | custom-call | tf_op jit(solution)/shard_map/triangular_solve/custom-call.8 | solution.py:119
  1692.8 22.5 %all-gather.35.cloned.1.call-done = f32[512,1024]{0,1:T(8,128)} async-done(((f32[128,1024]{0,1:T(8,128)}), f32[512,1024]{0,1:T(8,128)}) %all-gather.35.cloned.1.call-update) | async-done | bytes 2097168 | tf_op jit(solution)/shard_map/all_gather | solution.py:130
  (592 shorter events, 904.0 us)
Async XLA Ops:
  7.2 30.2 %all-gather.15.cloned.1.call-start = ((), (), s32[]{:S(2)}) async-start(), calls=%async_computation.1 | async-start | bytes 1310720 | tf_op jit(solution)/shard_map/all_gather | solution.py:110
  7.2 1.8 collective-permute-start
  10.9 52.5 %all-gather.13.cloned.1.call-start = ((), (), s32[]{:S(2)}) async-start(), calls=%async_computation | async-start | bytes 1310720 | tf_op jit(solution)/shard_map/all_gather | solution.py:109
  14.4 59.2 %collective-permute-start.1 = (f32[3,256,1024]{1,2,0:T(8,128)}, f32[3,256,1024]{1,2,0:T(8,128)}, u32[]{:S(2)}, u32[]{:S(2)}) collective-permute-start(f32[3,256,1024]{1,2,0:T(8,128)} %bitcast.5), channel_id=1, source_target_pairs={{0,4},{4,0},{8,12},{12,8},{16,20},{20,16},{24,28},{28,24},{32,36},... | collective-permute-start | bytes 9437192 | tf_op jit(solution)/shard_map/ppermute | solution.py:12
  14.6 113.3 %all-gather.17.cloned.1.call-start = ((), (), s32[]{:S(2)}) async-start(), calls=%async_computation.2 | async-start | bytes 5242880 | tf_op jit(solution)/shard_map/all_gather | solution.py:117
  79.2 514.7 %all-gather.19.cloned.1.call-start = ((), (), s32[]{:S(2)}) async-start(), calls=%async_computation.3 | async-start | bytes 2621440 | tf_op jit(solution)/shard_map/all_gather | solution.py:130
  82.3 3.8 collective-permute-start.2
  558.9 52.4 %copy-start.39 = (s32[384]{0:T(512)S(1)}, s32[384]{0:T(512)}, u32[]{:S(2)}) copy-start(s32[384]{0:T(512)} %get-tuple-element.75) | copy-start | bytes 4612
  558.9 52.4 %copy-start.40 = (s32[384]{0:T(512)S(1)}, s32[384]{0:T(512)}, u32[]{:S(2)}) copy-start(s32[384]{0:T(512)} %get-tuple-element.76) | copy-start | bytes 4612
  558.9 52.5 %copy-start.37 = (s32[384]{0:T(512)S(1)}, s32[384]{0:T(512)}, u32[]{:S(2)}) copy-start(s32[384]{0:T(512)} %get-tuple-element.73) | copy-start | bytes 4612
  558.9 52.5 %copy-start.38 = (s32[384]{0:T(512)S(1)}, s32[384]{0:T(512)}, u32[]{:S(2)}) copy-start(s32[384]{0:T(512)} %get-tuple-element.74) | copy-start | bytes 4612
  558.9 99.9 %all-gather.23.cloned.1.call-start = ((), (), s32[]{:S(2)}) async-start(), calls=%async_computation.5 | async-start | bytes 1310720 | tf_op jit(solution)/shard_map/all_gather | solution.py:110
  599.1 7.4 collective-permute-start.3
  608.3 55.4 %all-gather.21.cloned.1.call-start = ((), (), s32[]{:S(2)}) async-start(), calls=%async_computation.4 | async-start | bytes 1310720 | tf_op jit(solution)/shard_map/all_gather | solution.py:109
  609.8 45.9 %collective-permute-start.4 = (f32[2,256,1024]{1,2,0:T(8,128)}, f32[2,256,1024]{1,2,0:T(8,128)}, u32[]{:S(2)}, u32[]{:S(2)}) collective-permute-start(f32[2,256,1024]{1,2,0:T(8,128)} %slice.559), channel_id=1, source_target_pairs={{0,8},{4,12},{8,0},{12,4},{16,24},{20,28},{24,16},{28,20},{32,40},... | collective-permute-start | bytes 6291464 | tf_op jit(solution)/shard_map/ppermute | solution.py:12
  611.3 116.2 %all-gather.25.cloned.1.call-start = ((), (), s32[]{:S(2)}) async-start(), calls=%async_computation.6 | async-start | bytes 5242880 | tf_op jit(solution)/shard_map/all_gather | solution.py:117
  678.1 479.8 %all-gather.27.cloned.1.call-start = ((), (), s32[]{:S(2)}) async-start(), calls=%async_computation.7 | async-start | bytes 2621440 | tf_op jit(solution)/shard_map/all_gather | solution.py:130
  680.4 24.2 %collective-permute-start.5 = (f32[2,128,1024]{1,2,0:T(8,128)}, f32[2,128,1024]{1,2,0:T(8,128)S(1)}, u32[]{:S(2)}, u32[]{:S(2)}) collective-permute-start(f32[2,128,1024]{1,2,0:T(8,128)} %slice.576), channel_id=1, source_target_pairs={{0,8},{4,12},{8,0},{12,4},{16,24},{20,28},{24,16},{28,20},{32,40},... | collective-permute-start | bytes 3145736 | tf_op jit(solution)/shard_map/ppermute | solution.py:12
  893.3 29.3 %copy-start.17 = (f32[512,512]{1,0:T(8,128)}, f32[512,512]{1,0:T(8,128)S(1)}, u32[]{:S(2)}) copy-start(f32[512,512]{1,0:T(8,128)S(1)} %convolution_subtract_fusion.1) | copy-start | bytes 3145732
  994.0 109.5 %copy-start.22 = (f32[128,1024]{0,1:T(8,128)S(1)}, f32[128,1024]{0,1:T(8,128)}, u32[]{:S(2)}) copy-start(f32[128,1024]{0,1:T(8,128)} %fusion.50) | copy-start | bytes 1572868
  1115.5 57.8 %copy-start.35 = (s32[384]{0:T(512)S(1)}, s32[384]{0:T(512)}, u32[]{:S(2)}) copy-start(s32[384]{0:T(512)} %get-tuple-element.77) | copy-start | bytes 4612
  1115.5 57.8 %copy-start.36 = (s32[384]{0:T(512)S(1)}, s32[384]{0:T(512)}, u32[]{:S(2)}) copy-start(s32[384]{0:T(512)} %get-tuple-element.78) | copy-start | bytes 4612
  1115.5 57.9 %copy-start.33 = (s32[384]{0:T(512)S(1)}, s32[384]{0:T(512)}, u32[]{:S(2)}) copy-start(s32[384]{0:T(512)} %get-tuple-element.59) | copy-start | bytes 4612
  1115.5 57.9 %copy-start.34 = (s32[384]{0:T(512)S(1)}, s32[384]{0:T(512)}, u32[]{:S(2)}) copy-start(s32[384]{0:T(512)} %get-tuple-element.60) | copy-start | bytes 4612
  1122.9 76.8 %all-gather.31.cloned.1.call-start = ((), (), s32[]{:S(2)}) async-start(), calls=%async_computation.9 | async-start | bytes 1310720 | tf_op jit(solution)/shard_map/all_gather | solution.py:110
  1163.0 8.8 collective-permute-start.6
  1172.7 55.3 %all-gather.29.cloned.1.call-start = ((), (), s32[]{:S(2)}) async-start(), calls=%async_computation.8 | async-start | bytes 1310720 | tf_op jit(solution)/shard_map/all_gather | solution.py:109
  1173.3 124.6 %all-gather.33.cloned.1.call-start = ((), (), s32[]{:S(2)}) async-start(), calls=%async_computation.10 | async-start | bytes 5242880 | tf_op jit(solution)/shard_map/all_gather | solution.py:117
  1174.5 71.3 %collective-permute-start.7 = (f32[1,256,1024]{1,2,0:T(8,128)}, f32[1,256,1024]{1,2,0:T(8,128)}, u32[]{:S(2)}, u32[]{:S(2)}) collective-permute-start(f32[1,256,1024]{1,2,0:T(8,128)} %slice.601), channel_id=1, source_target_pairs={{0,16},{4,20},{8,24},{12,28},{16,0},{20,4},{24,8},{28,12},{32,48},... | collective-permute-start | bytes 3145736 | tf_op jit(solution)/shard_map/ppermute | solution.py:12
  1248.5 466.9 %all-gather.35.cloned.1.call-start = ((), (), s32[]{:S(2)}) async-start(), calls=%async_computation.11 | async-start | bytes 2621440 | tf_op jit(solution)/shard_map/all_gather | solution.py:130
  1248.6 14.4 collective-permute-start.8
  1560.2 107.5 %copy-start.23 = (f32[128,1024]{0,1:T(8,128)S(1)}, f32[128,1024]{0,1:T(8,128)}, u32[]{:S(2)}) copy-start(f32[128,1024]{0,1:T(8,128)} %slice_add_fusion.1) | copy-start | bytes 1572868
  (40 other events, 239.5 us)
Sparse Core Ops, SparseCore 0:
  11.0 26.3 all-gather.14
  39.1 24.2 all-gather.12
  79.4 48.5 all-gather.16
  559.0 34.8 all-gather.18
  608.4 26.8 all-gather.22
  636.8 26.8 all-gather.20
  678.3 49.1 all-gather.24
  1123.0 34.8 all-gather.26
  1172.8 26.8 all-gather.30
  1201.2 26.8 all-gather.28
  1248.7 49.1 all-gather.32
  1680.5 34.8 all-gather.34
where the time goes:
time: 1740 us; the launch traced here: 1730 us
  other arithmetic  934 us (54%)
  waiting for transfers between devices  364 us (21%)
  local copies, waits for them, and re-layouts  221 us (13%)
  matrix products  163 us (9%)
  between operations  31.4 us (2%)
    another operation x90, other arithmetic, block_cholesky(): return jnp.linalg.cholesky(matrix, symmetrize_input=False)  494 us
    another operation x5, other arithmetic, on_device(): lax.linalg.triangular_solve(pivot_factor, front_below, left_side=False, l...  245 us
    another operation x7, other arithmetic, block_cholesky(): lax.linalg.triangular_solve(top_factor, matrix[half:, :half], left_side=F...  124 us
    ppermute x9, waiting for transfers between devices, partner(): lax.ppermute(x, axis, [(i, i ^ 1 << stride) for i in range(lax.axis_size(...  94.6 us
    all_gather x3, waiting for transfers between devices, on_device(): lax.all_gather(solved, 'rows', axis=0, tiled=True)  92.4 us
    all_gather x3, waiting for transfers between devices, on_device(): pivot_block = lax.all_gather(front_pivot, 'rows', axis=0, tiled=True)  88.2 us
    another operation x76, local copies, waits for them, and re-layouts, on_device(): lax.linalg.triangular_solve(pivot_factor, front_below, left_side=False, l...  75.5 us
    another operation x45, matrix products, on_device(): lax.linalg.triangular_solve(pivot_factor, front_below, left_side=False, l...  53.7 us
  transfers between devices with their start and end apart: 21, of which 18 were waited for; matrix products, arithmetic and copies ran while one was open for 5% of the time, Pallas kernels for 0%

commit v1 on v0

--- a/solution.py
+++ b/solution.py
@@ -6,6 +6,28 @@
 BLK = 128
 LEVELS = 3
 highest = lax.Precision.HIGHEST
+
+
+def in_order(blocks, dim):
+    blocks = jnp.moveaxis(blocks, 0, dim)
+    shape = blocks.shape
+    return blocks.reshape(*shape[:dim], shape[dim] * shape[dim + 1], *shape[dim + 2 :])
+
+
+def gather_around(x, axis, dim):
+    peers = lax.axis_size(axis)
+    pairs = [(i, (i + 1) % peers) for i in range(peers)]
+    back = [(b, a) for a, b in pairs]
+    lower, upper = ([], [])
+    for hop in range(peers - 1):
+        if hop % 2 == 0:
+            lower.append(lax.ppermute(lower[-1] if lower else x, axis, pairs))
+        else:
+            upper.append(lax.ppermute(upper[-1] if upper else x, axis, back))
+    pieces = jnp.stack([*lower[::-1], x, *upper])
+    shift = lax.axis_index(axis) - len(lower)
+    pieces = pieces[(jnp.arange(peers) - shift) % peers]
+    return in_order(pieces, dim)
 
 
 def partner(x, axis, stride):
@@ -107,7 +129,7 @@
             jnp.zeros((sep_rows + upd_rows, front_width), jnp.float32),
             (
                 lax.all_gather(left_rows, "rows", axis=0, tiled=True),
-                lax.all_gather(right_rows, "rows", axis=0, tiled=True),
+                gather_around(right_rows, "rows", 0),
             ),
             jnp.int32(0),
         )

time: 1740 us -> 1670 us (0.960)
  waiting for transfers between devices: 364 us -> 285 us
    all_gather x3 -> x0, waiting for transfers between devices: 43.6 us -> none  [on_device(): lax.all_gather(right_rows, 'rows', axis=0, tiled=True)]
    ppermute x0 -> x9, waiting for transfers between devices: none -> 41.3 us  [the longest x6 41.3 us: gather_around(): lower.append(lax.ppermute(lower[-1] if lower else x, axis, pairs))]
    ppermute x9, waiting for transfers between devices: 94.6 us -> 56.4 us  [partner(): lax.ppermute(x, axis, [(i, i ^ 1 << stride) for i in range(lax.axis_size(...]
    all_gather x3, waiting for transfers between devices: 44.4 us -> 8.17 us  [on_device(): lax.all_gather(left_rows, 'rows', axis=0, tiled=True)]
  transfers between devices with their start and end apart: 21 -> 27, of which waited for: 18 -> 19; matrix products, arithmetic and copies ran while one was open for 5% -> 5% of each run, Pallas kernels for 0% -> 0%
where the time goes in v1:
time: 1670 us; the launch traced here: 1660 us
  other arithmetic  933 us (56%)
  waiting for transfers between devices  285 us (17%)
  local copies, waits for them, and re-layouts  222 us (13%)
  matrix products  163 us (10%)
  between operations  31.5 us (2%)
  starting transfers between devices  25.2 us (2%)
    another operation x90, other arithmetic, block_cholesky(): return jnp.linalg.cholesky(matrix, symmetrize_input=False)  494 us
    another operation x5, other arithmetic, on_device(): lax.linalg.triangular_solve(pivot_factor, front_below, left_side=False, l...  245 us
    another operation x7, other arithmetic, block_cholesky(): lax.linalg.triangular_solve(top_factor, matrix[half:, :half], left_side=F...  124 us
    all_gather x3, waiting for transfers between devices, on_device(): lax.all_gather(solved, 'rows', axis=0, tiled=True)  89.4 us
    all_gather x3, waiting for transfers between devices, on_device(): pivot_block = lax.all_gather(front_pivot, 'rows', axis=0, tiled=True)  89.3 us
    another operation x76, local copies, waits for them, and re-layouts, on_device(): lax.linalg.triangular_solve(pivot_factor, front_below, left_side=False, l...  75.5 us
    ppermute x9, waiting for transfers between devices, partner(): lax.ppermute(x, axis, [(i, i ^ 1 << stride) for i in range(lax.axis_size(...  56.4 us
    another operation x45, matrix products, on_device(): lax.linalg.triangular_solve(pivot_factor, front_below, left_side=False, l...  53.7 us
  transfers between devices with their start and end apart: 27, of which 19 were waited for; matrix products, arithmetic and copies ran while one was open for 5% of the time, Pallas kernels for 0%

profile of v1, /device:TPU:0, one launch (start us, length us, event | category | flops | bytes accessed | tf_op | source)
XLA Modules:
  0.0 1660.6 jit_solution(15116284129828641770)
XLA Ops:
  23.4 13.5 collective-permute-done.2
  68.4 38.2 %all-gather.12.cloned.1.call-done = f32[1024,1024]{0,1:T(8,128)} async-done(((f32[256,1024]{0,1:T(8,128)}), f32[1024,1024]{0,1:T(8,128)}) %all-gather.12.cloned.1.call-update) | async-done | bytes 4194320 | tf_op jit(solution)/shard_map/all_gather | solution.py:139
  118.9 11.7 cholesky.645
  144.6 11.7 cholesky.665
  173.7 11.7 cholesky.686
  198.9 12.1 cholesky.703
  217.7 11.9 while.12
  230.3 40.1 %custom-call.48 = f32[4,128,128]{1,2,0:T(8,128)S(1)} custom-call(f32[4,128,128]{2,1,0:T(8,128)} %copy-done.33), custom_call_target="InvertDiagBlocksLowerTriangular" | custom-call | tf_op jit(solution)/shard_map/triangular_solve/custom-call.3 | solution.py:43
  288.4 11.7 cholesky.718
  318.8 12.5 cholesky.738
  350.9 13.2 cholesky.759
  405.4 28.5 %while.13 = (s32[]{:T(128)}, f32[1024,1024]{1,0:T(8,128)}, s32[8,2]{0,1:T(2,128)S(1)}, f32[8,128,128]{2,1,0:T(8,128)}, s32[]{:T(128)}) while((s32[]{:T(128)}, f32[1024,1024]{1,0:T(8,128)}, s32[8,2]{0,1:T(2,128)S(1)}, f32[8,128,128]{2,1,0:T(8,128)}, s32[]{:T(128)}) %tuple.251), condition=%wide.while_cond.1, body=%wide.while_body.1.sunk | while | flops 2 | bytes 132205 | solution.py:141
  433.9 80.4 %custom-call.52 = f32[8,128,128]{1,2,0:T(8,128)} custom-call(f32[8,128,128]{2,1,0:T(8,128)} %get-tuple-element.48), custom_call_target="InvertDiagBlocksLowerTriangular" | custom-call | tf_op jit(solution)/shard_map/triangular_solve/custom-call.8 | solution.py:141
  541.0 31.9 %all-gather.14.cloned.1.call-done = f32[512,1024]{0,1:T(8,128)} async-done(((f32[128,1024]{0,1:T(8,128)}), f32[512,1024]{0,1:T(8,128)}) %all-gather.14.cloned.1.call-update) | async-done | bytes 2097168 | tf_op jit(solution)/shard_map/all_gather | solution.py:152
  579.7 13.1 collective-permute-done.6
  640.9 22.9 %collective-permute-done.11 = f32[2,128,1024]{1,2,0:T(8,128)S(1)} collective-permute-done((f32[2,128,1024]{1,2,0:T(8,128)}, f32[2,128,1024]{1,2,0:T(8,128)S(1)}, u32[]{:S(2)}, u32[]{:S(2)}) %collective-permute-start.11) | collective-permute-done | bytes 1048608 | tf_op jit(solution)/shard_map/ppermute | solution.py:34
  668.0 18.5 %all-gather.18.cloned.1.call-done = f32[1024,1024]{0,1:T(8,128)} async-done(((f32[256,1024]{0,1:T(8,128)}), f32[1024,1024]{0,1:T(8,128)}) %all-gather.18.cloned.1.call-update) | async-done | bytes 4194320 | tf_op jit(solution)/shard_map/all_gather | solution.py:139
  723.5 12.3 cholesky.811
  773.8 11.9 cholesky.849
  790.6 12.0 while.14
  802.7 39.3 %custom-call.56 = f32[4,128,128]{1,2,0:T(8,128)S(1)} custom-call(f32[4,128,128]{2,1,0:T(8,128)S(1)} %get-tuple-element.49), custom_call_target="InvertDiagBlocksLowerTriangular" | custom-call | tf_op jit(solution)/shard_map/triangular_solve/custom-call.3 | solution.py:43
  882.8 12.5 cholesky.884
  910.1 13.2 cholesky.905
  960.8 23.2 %while.15 = (s32[]{:T(128)}, f32[1024,1024]{1,0:T(8,128)}, s32[8,2]{0,1:T(2,128)S(1)}, f32[8,128,128]{2,1,0:T(8,128)S(1)}, s32[]{:T(128)}) while((s32[]{:T(128)}, f32[1024,1024]{1,0:T(8,128)}, s32[8,2]{0,1:T(2,128)S(1)}, f32[8,128,128]{2,1,0:T(8,128)S(1)}, s32[]{:T(128)}) %tuple.286), condition=%wide.while_cond.1.clone, body=%wide.while_body.1.clone.sunk | while | flops 2 | bytes 131189 | solution.py:141
  984.1 79.4 %custom-call.60 = f32[8,128,128]{1,2,0:T(8,128)} custom-call(f32[8,128,128]{2,1,0:T(8,128)S(1)} %get-tuple-element.50), custom_call_target="InvertDiagBlocksLowerTriangular" | custom-call | tf_op jit(solution)/shard_map/triangular_solve/custom-call.8 | solution.py:141
  1082.9 35.0 %all-gather.20.cloned.1.call-done = f32[512,1024]{0,1:T(8,128)} async-done(((f32[128,1024]{0,1:T(8,128)}), f32[512,1024]{0,1:T(8,128)}) %all-gather.20.cloned.1.call-update) | async-done | bytes 2097168 | tf_op jit(solution)/shard_map/all_gather | solution.py:152
  1198.0 32.7 %all-gather.24.cloned.1.call-done = f32[1024,1024]{0,1:T(8,128)} async-done(((f32[256,1024]{0,1:T(8,128)}), f32[1024,1024]{0,1:T(8,128)}) %all-gather.24.cloned.1.call-update) | async-done | bytes 4194320 | tf_op jit(solution)/shard_map/all_gather | solution.py:139
  1326.1 11.9 cholesky.995
  1353.9 39.3 %custom-call.64 = f32[4,128,128]{1,2,0:T(8,128)S(1)} custom-call(f32[4,128,128]{2,1,0:T(8,128)S(1)} %get-tuple-element.51), custom_call_target="InvertDiagBlocksLowerTriangular" | custom-call | tf_op jit(solution)/shard_map/triangular_solve/custom-call.3 | solution.py:43
  1498.4 23.2 %while.17 = (s32[]{:T(128)}, f32[1024,1024]{1,0:T(8,128)}, s32[8,2]{0,1:T(2,128)S(1)}, f32[8,128,128]{2,1,0:T(8,128)S(1)}, s32[]{:T(128)}) while((s32[]{:T(128)}, f32[1024,1024]{1,0:T(8,128)}, s32[8,2]{0,1:T(2,128)S(1)}, f32[8,128,128]{2,1,0:T(8,128)S(1)}, s32[]{:T(128)}) %tuple.287), condition=%wide.while_cond.1.clone.1, body=%wide.while_body.1.clone.1.sunk | while | flops 2 | bytes 131189 | solution.py:141
  1521.6 78.8 %custom-call.68 = f32[8,128,128]{1,2,0:T(8,128)S(1)} custom-call(f32[8,128,128]{2,1,0:T(8,128)S(1)} %get-tuple-element.52), custom_call_target="InvertDiagBlocksLowerTriangular" | custom-call | tf_op jit(solution)/shard_map/triangular_solve/custom-call.8 | solution.py:141
  1625.5 22.5 %all-gather.26.cloned.1.call-done = f32[512,1024]{0,1:T(8,128)} async-done(((f32[128,1024]{0,1:T(8,128)}), f32[512,1024]{0,1:T(8,128)}) %all-gather.26.cloned.1.call-update) | async-done | bytes 2097168 | tf_op jit(solution)/shard_map/all_gather | solution.py:152
  (615 shorter events, 908.1 us)
Async XLA Ops:
  7.2 33.4 %all-gather.10.cloned.1.call-start = ((), (), s32[]{:S(2)}) async-start(), calls=%async_computation | async-start | bytes 1310720 | tf_op jit(solution)/shard_map/all_gather | solution.py:131
  7.2 4.1 collective-permute-start
  10.9 40.0 %collective-permute-start.4 = (f32[3,256,1024]{1,2,0:T(8,128)}, f32[3,256,1024]{1,2,0:T(8,128)}, u32[]{:S(2)}, u32[]{:S(2)}) collective-permute-start(f32[3,256,1024]{1,2,0:T(8,128)} %bitcast.11), channel_id=1, source_target_pairs={{0,4},{4,0},{8,12},{12,8},{16,20},{20,16},{24,28},{28,24},{32,36},... | collective-permute-start | bytes 9437192 | tf_op jit(solution)/shard_map/ppermute | solution.py:34
  12.2 94.4 %all-gather.12.cloned.1.call-start = ((), (), s32[]{:S(2)}) async-start(), calls=%async_computation.1 | async-start | bytes 5242880 | tf_op jit(solution)/shard_map/all_gather | solution.py:139
  13.5 9.5 collective-permute-start.1
  15.2 8.2 collective-permute-start.3
  23.0 13.9 collective-permute-start.2
  56.5 516.5 %all-gather.14.cloned.1.call-start = ((), (), s32[]{:S(2)}) async-start(), calls=%async_computation.2 | async-start | bytes 2621440 | tf_op jit(solution)/shard_map/all_gather | solution.py:152
  59.5 3.8 collective-permute-start.5
  538.0 84.5 %all-gather.16.cloned.1.call-start = ((), (), s32[]{:S(2)}) async-start(), calls=%async_computation.3 | async-start | bytes 1310720 | tf_op jit(solution)/shard_map/all_gather | solution.py:131
  539.5 63.9 %collective-permute-start.10 = (f32[2,256,1024]{1,2,0:T(8,128)}, f32[2,256,1024]{1,2,0:T(8,128)}, u32[]{:S(2)}, u32[]{:S(2)}) collective-permute-start(f32[2,256,1024]{1,2,0:T(8,128)} %slice.565), channel_id=1, source_target_pairs={{0,8},{4,12},{8,0},{12,4},{16,24},{20,28},{24,16},{28,20},{32,40},... | collective-permute-start | bytes 6291464 | tf_op jit(solution)/shard_map/ppermute | solution.py:34
  578.1 14.7 collective-permute-start.6
  594.6 91.8 %all-gather.18.cloned.1.call-start = ((), (), s32[]{:S(2)}) async-start(), calls=%async_computation.4 | async-start | bytes 5242880 | tf_op jit(solution)/shard_map/all_gather | solution.py:139
  594.7 8.7 collective-permute-start.7
  595.7 11.0 collective-permute-start.9
  603.4 10.6 collective-permute-start.8
  637.1 480.8 %all-gather.20.cloned.1.call-start = ((), (), s32[]{:S(2)}) async-start(), calls=%async_computation.5 | async-start | bytes 2621440 | tf_op jit(solution)/shard_map/all_gather | solution.py:152
  639.4 24.4 %collective-permute-start.11 = (f32[2,128,1024]{1,2,0:T(8,128)}, f32[2,128,1024]{1,2,0:T(8,128)S(1)}, u32[]{:S(2)}, u32[]{:S(2)}) collective-permute-start(f32[2,128,1024]{1,2,0:T(8,128)} %slice.582), channel_id=1, source_target_pairs={{0,8},{4,12},{8,0},{12,4},{16,24},{20,28},{24,16},{28,20},{32,40},... | collective-permute-start | bytes 3145736 | tf_op jit(solution)/shard_map/ppermute | solution.py:34
  954.2 109.3 %copy-start.22 = (f32[128,1024]{0,1:T(8,128)S(1)}, f32[128,1024]{0,1:T(8,128)}, u32[]{:S(2)}) copy-start(f32[128,1024]{0,1:T(8,128)} %fusion.50) | copy-start | bytes 1572868
  1074.1 59.4 %copy-start.37 = (s32[384]{0:T(512)S(1)}, s32[384]{0:T(512)}, u32[]{:S(2)}) copy-start(s32[384]{0:T(512)} %get-tuple-element.62) | copy-start | bytes 4612
  1074.1 66.2 %copy-start.35 = (s32[384]{0:T(512)S(1)}, s32[384]{0:T(512)}, u32[]{:S(2)}) copy-start(s32[384]{0:T(512)} %get-tuple-element.80) | copy-start | bytes 4612
  1074.1 66.2 %copy-start.36 = (s32[384]{0:T(512)S(1)}, s32[384]{0:T(512)}, u32[]{:S(2)}) copy-start(s32[384]{0:T(512)} %get-tuple-element.81) | copy-start | bytes 4612
  1082.9 77.9 %all-gather.22.cloned.1.call-start = ((), (), s32[]{:S(2)}) async-start(), calls=%async_computation.6 | async-start | bytes 1310720 | tf_op jit(solution)/shard_map/all_gather | solution.py:131
  1123.1 8.8 collective-permute-start.12
  1132.6 98.1 %all-gather.24.cloned.1.call-start = ((), (), s32[]{:S(2)}) async-start(), calls=%async_computation.7 | async-start | bytes 5242880 | tf_op jit(solution)/shard_map/all_gather | solution.py:139
  1132.6 7.7 collective-permute-start.13
  1133.5 10.9 collective-permute-start.15
  1140.3 9.0 collective-permute-start.14
  1141.4 37.2 %collective-permute-start.16 = (f32[1,256,1024]{1,2,0:T(8,128)}, f32[1,256,1024]{1,2,0:T(8,128)}, u32[]{:S(2)}, u32[]{:S(2)}) collective-permute-start(f32[1,256,1024]{1,2,0:T(8,128)} %slice.607), channel_id=1, source_target_pairs={{0,16},{4,20},{8,24},{12,28},{16,0},{20,4},{24,8},{28,12},{32,48},... | collective-permute-start | bytes 3145736 | tf_op jit(solution)/shard_map/ppermute | solution.py:34
  1181.3 466.7 %all-gather.26.cloned.1.call-start = ((), (), s32[]{:S(2)}) async-start(), calls=%async_computation.8 | async-start | bytes 2621440 | tf_op jit(solution)/shard_map/all_gather | solution.py:152
  1181.4 14.7 collective-permute-start.17
  1492.9 107.5 %copy-start.23 = (f32[128,1024]{0,1:T(8,128)S(1)}, f32[128,1024]{0,1:T(8,128)}, u32[]{:S(2)}) copy-start(f32[128,1024]{0,1:T(8,128)} %slice_add_fusion.1) | copy-start | bytes 1572868
  (49 other events, 495.1 us)
Sparse Core Ops, SparseCore 0:
  12.3 28.1 all-gather.9
  56.6 49.9 all-gather.11
  538.1 34.8 all-gather.13
  594.7 27.7 all-gather.15
  637.2 49.1 all-gather.17
  1083.0 34.8 all-gather.19
  1132.7 28.0 all-gather.21
  1181.4 49.1 all-gather.23
  1613.2 34.8 all-gather.25
